TPU v7x, 32 devices: a whole 2x2x4 slice. The times are simulated.
32 devices in a mesh: groups: 2 (over y), frame: 4 (over z), query: 2 (over x), chan: 2 (over core).
Axes of the slice: x: 2, y: 2, z: 4, core: 2. Of those that a mesh axis runs over, the one named last changes fastest.
Arguments:
- features: bfloat16 [8, 64, 64, 256], P(('groups', 'frame'), None, None, 'chan'), parts along dimension 0, may hold values from -6 to 6
- query_frame: int32 [256], P(('groups', 'query')), parts along dimension 0, may hold values from 0 to 3
- query_pixel: int32 [256, 2], P(('groups', 'query')), parts along dimension 0, may hold values from 0 to 63
- conv_first: bfloat16 [3, 3, 1, 16], replicated, may hold values from -2 to 2
- conv_second: bfloat16 [3, 3, 16, 32], replicated, may hold values from -0.5 to 0.5
- depth_kernel: float32 [2, 3, 512], replicated, may hold values from -3 to 3
- w_in: bfloat16 [2, 2048, 512], P(None, ('frame', 'chan')), may hold values from -0.25 to 0.25
- w_out: bfloat16 [2, 2048, 512], P(None, ('frame', 'chan')), may hold values from -0.125 to 0.125
Outputs:
- tracks: bfloat16 [256, 4, 512], P(('groups', 'query'), 'frame'), parts along dimension 0
There are 2 independent parts, one for each index of `groups`. A program takes and returns all parts, laid end to end along the dimension named above; an argument that names none is the same for every part. Nothing has to cross between parts.
All inputs are finite; a program needn't handle non-finite values.
Results may differ from a plain program's by a relative error of at most 0.02.
Values may be sent and summed in bfloat16 or wider, within the bound.
A program may use at most 64 MiB of HBM per device.

v0:
```python
import math

import jax
import jax.numpy as jnp
from jax import lax
from jax.sharding import PartitionSpec as P

MIXERS = 2


def padded_2(block, sides, width):
    for axis, dim in sides:
        count = lax.axis_size(axis)
        forward = [(i, i + 1) for i in range(count - 1)]
        backward = [(target, source) for source, target in forward]
        low = lax.ppermute(
            lax.slice_in_dim(block, block.shape[dim] - width, None, axis=dim), axis, forward
        )
        high = lax.ppermute(lax.slice_in_dim(block, 0, width, axis=dim), axis, backward)
        block = jnp.concatenate([low, block, high], axis=dim)
    return block


def pool_maps(corr_maps, conv_first, conv_second):
    first_maps = lax.conv_general_dilated(
        corr_maps,
        conv_first,
        (2, 2),
        "SAME",
        dimension_numbers=("HWCN", "HWIO", "HWCN"),
        preferred_element_type=jnp.float32,
    )
    first_maps = jax.nn.relu(first_maps).astype(jnp.bfloat16)
    second_maps = lax.conv_general_dilated(
        first_maps,
        conv_second,
        (2, 2),
        "SAME",
        dimension_numbers=("HWCN", "HWIO", "HWCN"),
        preferred_element_type=jnp.float32,
    )
    second_maps = jax.nn.relu(second_maps)
    window = second_maps.shape[0] // 4
    pooled = second_maps.reshape(
        4, window, 4, window, second_maps.shape[2], second_maps.shape[3]
    ).mean(axis=(1, 3))
    return pooled.reshape(16 * second_maps.shape[2], second_maps.shape[3]).T


def layer_norm(state):
    centre = state - jnp.mean(state, axis=-1, keepdims=True)
    spread = jnp.mean(centre * centre, axis=-1, keepdims=True)
    return (centre * lax.rsqrt(spread + 1e-05)).astype(jnp.bfloat16)


def depth_mix(padded, kernel):
    length = padded.shape[1] - 2
    wide = padded.astype(jnp.float32)
    summed = (
        kernel[0] * wide[:, :length] + kernel[1] * wide[:, 1 : length + 1] + kernel[2] * wide[:, 2:]
    )
    return summed.astype(jnp.bfloat16)


def on_device(
    features, query_frame, query_pixel, conv_first, conv_second, depth_kernel, w_in, w_out
):
    frame_count = features.shape[0]
    side_cells = features.shape[1]
    chan_width = features.shape[3]
    row_ids = query_pixel[:, 0]
    col_ids = query_pixel[:, 1]
    local_frame = query_frame - lax.axis_index("frame") * frame_count
    owned_mask = ((local_frame >= 0) & (local_frame < frame_count)).astype(jnp.float32)
    picked = features[jnp.clip(local_frame, 0, frame_count - 1), row_ids, col_ids, :].astype(
        jnp.float32
    )
    picked = picked * owned_mask[:, None]
    query_vectors = lax.psum(picked.astype(jnp.bfloat16), "frame")
    corr_scale = 1.0 / math.sqrt(chan_width * lax.axis_size("chan"))
    flat = features.reshape(frame_count * side_cells * side_cells, chan_width)
    local_corr = jnp.dot(flat, query_vectors.T, preferred_element_type=jnp.float32)
    summed = lax.psum_scatter(
        local_corr.astype(jnp.bfloat16), "chan", scatter_dimension=1, tiled=True
    ).astype(jnp.float32)
    corr_maps = (
        (summed * corr_scale)
        .astype(jnp.bfloat16)
        .reshape(frame_count, side_cells, side_cells, 1, summed.shape[1])
    )
    pooled = lax.map(lambda frame_maps: pool_maps(frame_maps, conv_first, conv_second), corr_maps)
    state = jnp.transpose(pooled, (1, 0, 2))
    for mixer in range(MIXERS):
        normed = layer_norm(state)
        padded = padded_2(normed, (("frame", 1),), 1)
        mixed = depth_mix(padded, depth_kernel[mixer])
        row_block = mixed.reshape(-1, mixed.shape[2])
        empty = jnp.zeros(row_block.shape, jnp.float32)
        in_piece = lax.all_gather(w_in[mixer], ("frame", "chan"), axis=0, tiled=True)
        out_piece = lax.all_gather(w_out[mixer], ("frame", "chan"), axis=0, tiled=True)
        pre_act = lax.dot_general(
            row_block, in_piece, (((1,), (1,)), ((), ())), preferred_element_type=jnp.float32
        )
        hidden = jax.nn.gelu(pre_act, approximate=False).astype(jnp.bfloat16)
        update = empty + jnp.dot(hidden, out_piece, preferred_element_type=jnp.float32)
        state = state + update.reshape(state.shape)
    tracks = state.astype(jnp.bfloat16)
    tracks = lax.all_gather(tracks, "chan", axis=0, tiled=True)
    return tracks


def solution(mesh):
    in_specs = (
        P(("groups", "frame"), None, None, "chan"),
        P(("groups", "query")),
        P(("groups", "query"), None),
        P(),
        P(),
        P(),
        P(None, ("frame", "chan"), None),
        P(None, ("frame", "chan"), None),
    )
    out_specs = P(("groups", "query"), "frame", None)
    return jax.shard_map(
        on_device, mesh=mesh, in_specs=in_specs, out_specs=out_specs, check_vma=False
    )
```

profile of v0, /device:TPU:0, one launch (start us, length us, event | category | flops | bytes accessed | tf_op | source)
XLA Modules:
  0.0 164.9 jit_solution(18240802262996446110)
XLA Ops:
  7.4 0.8 and_convert_fusion
  8.2 0.8 fusion.145
  9.0 0.8 gather_fusion
  9.8 0.1 multiply_convert_fusion.3
  9.9 20.5 %psum.7 = bf16[64,128]{1,0:T(8,128)(2,1)S(1)} all-reduce(bf16[64,128]{1,0:T(8,128)(2,1)S(1)} %multiply_convert_fusion.3), channel_id=1, replica_groups=mesh['groups'=2,'frame'=4,'query'=2,'chan'=2] {'frame'}, use_global_device_ids=true, to_apply=%region_0.1 | all-reduce | flops 8192 | bytes 32768 | tf_op jit(solution)/shard_map/psum | solution.py:79
  30.4 1.3 fusion
  31.7 0.0 reduce-scatter.2.cloned.1.call-update
  31.7 0.0 all-gather.10.cloned.1.call-start
  31.8 0.9 fusion.208
  32.6 0.0 all-gather.10.cloned.1.call-update
  32.6 0.0 all-gather.12.cloned.1.call-start
  32.7 0.8 fusion.209
  33.6 0.0 all-gather.12.cloned.1.call-update
  33.6 0.0 all-gather.14.cloned.1.call-start
  33.6 0.5 all-gather.14.cloned.1.call-update
  34.2 0.0 all-gather.16.cloned.1.call-start
  34.2 0.0 copy-start.4
  34.2 0.0 copy-start.5
  34.2 0.7 all-gather.16.cloned.1.call-update
  34.9 3.1 %reduce-scatter.2.cloned.1.call-done = bf16[4096,32]{0,1:T(8,128)(2,1)} async-done(((bf16[4096,64]{0,1:T(8,128)(2,1)}), bf16[4096,32]{0,1:T(8,128)(2,1)}) %reduce-scatter.2.cloned.1.call-update) | async-done | bytes 262160 | tf_op jit(solution)/shard_map/reduce_scatter | solution.py:83
  38.0 1.0 multiply_convert_fusion
  39.0 1.3 squeeze.21
  40.4 4.8 %copy.11 = bf16[64,64,1,32]{3,2,1,0:T(2,128)(2,1)S(1)} copy(bf16[64,64,1,32]{1,0,3,2:T(8,128)(2,1)} %squeeze.21) | data formatting | bytes 524288 | tf_op jit(solution)/shard_map/while/body/jit(dynamic_index_in_dim)/squeeze | solution.py:91
  45.2 8.0 %fusion.5 = f32[16,16,32,32]{2,3,1,0:T(8,128)} fusion(bf16[3,3,16,32]{3,2,1,0:T(8,128)(2,1)S(1)} %copy-done.4, bf16[64,64,1,32]{3,2,1,0:T(2,128)(2,1)S(1)} %copy.11, bf16[3,3,1,16]{3,1,2,0:T(4,128)(2,1)S(1)} %copy-done.5), kind=kOutput, calls=%fused_computation.7 | convolution fusion | flops 82936832 | bytes 1320224 | tf_op jit(solution)/shard_map/while/body/eval_jaxpr/conv_general_dilated | solution.py:34
  53.2 2.8 %reduce_sum.46 = f32[4,4,32,32]{2,3,1,0:T(8,128)S(1)} reduce(f32[4,4,4,4,32,32]{4,5,3,2,1,0:T(8,128)} %bitcast.79, f32[]{:T(128)} %constant.16.clone.1), dimensions={1,3}, to_apply=%region_2.3 | reduce | flops 245760 | bytes 1114116 | tf_op jit(solution)/shard_map/while/body/eval_jaxpr/reduce_sum | solution.py:46
  56.0 0.1 fusion.207
  56.1 0.2 copy.13
  56.3 0.2 div.19
  56.5 0.2 multiply_reduce_fusion.1
  56.7 0.1 fusion.117
  56.8 3.6 %collective-permute-start = (bf16[32,1,512]{2,0,1:T(8,128)(2,1)S(1)}, bf16[32,1,512]{2,0,1:T(8,128)(2,1)S(1)}, u32[]{:S(2)}, u32[]{:S(2)}) collective-permute-start(bf16[32,1,512]{2,0,1:T(8,128)(2,1)S(1)} %fusion.117), channel_id=1, source_target_pairs={{0,4},{4,8},{8,12},{1,5},{5,9},{9,13},{2,6},{6,10},{10,14},{3,7},{... | collective-permute-start | bytes 98312 | tf_op jit(solution)/shard_map/ppermute | solution.py:16
  60.4 1.3 collective-permute-start.1
  61.7 0.2 collective-permute-done
  62.0 4.2 %collective-permute-done.1 = bf16[32,1,512]{2,0,1:T(8,128)(2,1)S(1)} collective-permute-done((bf16[32,1,512]{2,0,1:T(8,128)(2,1)S(1)}, bf16[32,1,512]{2,0,1:T(8,128)(2,1)S(1)}, u32[]{:S(2)}, u32[]{:S(2)}) %collective-permute-start.1) | collective-permute-done | bytes 32800 | tf_op jit(solution)/shard_map/ppermute | solution.py:19
  66.2 0.0 all-gather.10.cloned.1.call-done
  66.2 24.8 %all-gather.12.cloned.1.call-done = bf16[1,2048,512]{2,1,0:T(8,128)(2,1)} async-done(((bf16[1,256,512]{2,1,0:T(8,128)(2,1)}), bf16[1,2048,512]{2,1,0:T(8,128)(2,1)}) %all-gather.12.cloned.1.call-update) | async-done | bytes 2097168 | tf_op jit(solution)/shard_map/all_gather | solution.py:100
  91.0 3.6 %fusion.211 = (f32[32]{0:T(128)S(1)}, f32[32,512]{1,0:T(8,128)S(1)}) fusion(bf16[1,2048,512]{2,1,0:T(8,128)(2,1)} %all-gather.12.cloned.1.call-done, bf16[1,2048,512]{2,1,0:T(8,128)(2,1)} %all-gather.10.cloned.1.call-done, f32[32,3,512]{2,0,1:T(8,128)S(1)} %maximum_convert_fusion.4, f32[512]{0:T(512)S(1)} %bitcast.84, f32[512]{0:T(512)S(1)} %bitcast.85, ...), kind=kOutput, calls=%fused_computation.229 | convolution fusion | flops 138608608 | bytes 4528256 | tf_op jit(solution)/shard_map/dot_general | solution.py:105
  94.6 0.2 multiply_reduce_fusion
  94.8 0.1 fusion.118
  94.9 3.3 %collective-permute-start.2 = (bf16[32,1,512]{2,0,1:T(8,128)(2,1)S(1)}, bf16[32,1,512]{2,0,1:T(8,128)(2,1)S(1)}, u32[]{:S(2)}, u32[]{:S(2)}) collective-permute-start(bf16[32,1,512]{2,0,1:T(8,128)(2,1)S(1)} %fusion.118), channel_id=1, source_target_pairs={{0,4},{4,8},{8,12},{1,5},{5,9},{9,13},{2,6},{6,10},{10,14},{3,7},{... | collective-permute-start | bytes 98312 | tf_op jit(solution)/shard_map/ppermute | solution.py:16
  98.3 1.3 collective-permute-start.3
  99.6 0.3 collective-permute-done.2
  99.8 5.6 %collective-permute-done.3 = bf16[32,1,512]{2,0,1:T(8,128)(2,1)S(1)} collective-permute-done((bf16[32,1,512]{2,0,1:T(8,128)(2,1)S(1)}, bf16[32,1,512]{2,0,1:T(8,128)(2,1)S(1)}, u32[]{:S(2)}, u32[]{:S(2)}) %collective-permute-start.3) | collective-permute-done | bytes 32800 | tf_op jit(solution)/shard_map/ppermute | solution.py:19
  105.5 16.5 %all-gather.14.cloned.1.call-done = bf16[1,2048,512]{2,1,0:T(8,128)(2,1)} async-done(((bf16[1,256,512]{2,1,0:T(8,128)(2,1)}), bf16[1,2048,512]{2,1,0:T(8,128)(2,1)}) %all-gather.14.cloned.1.call-update) | async-done | bytes 2097168 | tf_op jit(solution)/shard_map/all_gather | solution.py:99
  122.0 29.3 %all-gather.16.cloned.1.call-done = bf16[1,2048,512]{2,1,0:T(8,128)(2,1)} async-done(((bf16[1,256,512]{2,1,0:T(8,128)(2,1)}), bf16[1,2048,512]{2,1,0:T(8,128)(2,1)}) %all-gather.16.cloned.1.call-update) | async-done | bytes 2097168 | tf_op jit(solution)/shard_map/all_gather | solution.py:100
  151.3 3.5 %fusion.20 = bf16[32,512]{1,0:T(8,128)(2,1)S(1)} fusion(f32[32,512]{1,0:T(8,128)S(1)} %get-tuple-element.33, bf16[1,2048,512]{2,1,0:T(8,128)(2,1)} %all-gather.16.cloned.1.call-done, bf16[1,2048,512]{2,1,0:T(8,128)(2,1)} %all-gather.14.cloned.1.call-done, f32[32,3,512]{2,0,1:T(8,128)S(1)} %maximum_convert_fusion.5, f32[512]{0:T(512)S(1)} %bitcast.82, ...), kind=kOutput, calls=%fused_computation.18 | convolution fusion | flops 138608640 | bytes 4495360 | tf_op jit(solution)/shard_map/dot_general | solution.py:105
  154.8 1.9 %all-gather.4 = bf16[64,512]{1,0:T(8,128)(2,1)S(1)} all-gather(bf16[32,512]{1,0:T(8,128)(2,1)S(1)} %fusion.20), channel_id=6, replica_groups=mesh['groups'=2,'frame'=4,'query'=2,'chan'=2] {'chan'}, dimensions={0}, use_global_device_ids=true | all-gather | bytes 98304 | tf_op jit(solution)/shard_map/all_gather | solution.py:108
  156.7 0.6 copy.18
  (18 shorter events, 0.1 us)
Async XLA Ops:
  7.4 1.6 copy-start
  7.4 24.4 %copy-start.1 = (bf16[2,256,512]{2,1,0:T(8,128)(2,1)S(1)}, bf16[2,256,512]{2,1,0:T(8,128)(2,1)}, u32[]{:S(2)}) copy-start(bf16[2,256,512]{2,1,0:T(8,128)(2,1)} %param.14) | copy-start | bytes 1572868
  7.4 25.3 %copy-start.2 = (bf16[2,256,512]{2,1,0:T(8,128)(2,1)S(1)}, bf16[2,256,512]{2,1,0:T(8,128)(2,1)}, u32[]{:S(2)}) copy-start(bf16[2,256,512]{2,1,0:T(8,128)(2,1)} %param.15) | copy-start | bytes 1572868
  7.4 30.6 %reduce-scatter.2.cloned.1.call-start = ((), (), s32[]{:S(2)}) async-start(), calls=%async_computation.1 | async-start | bytes 786432 | tf_op jit(solution)/shard_map/reduce_scatter | solution.py:83
  31.7 34.5 %all-gather.10.cloned.1.call-start = ((), (), s32[]{:S(2)}) async-start(), calls=%async_computation.2 | async-start | bytes 2359296 | tf_op jit(solution)/shard_map/all_gather | solution.py:99
  32.6 58.4 %all-gather.12.cloned.1.call-start = ((), (), s32[]{:S(2)}) async-start(), calls=%async_computation.3 | async-start | bytes 2359296 | tf_op jit(solution)/shard_map/all_gather | solution.py:100
  33.6 88.4 %all-gather.14.cloned.1.call-start = ((), (), s32[]{:S(2)}) async-start(), calls=%async_computation.4 | async-start | bytes 2359296 | tf_op jit(solution)/shard_map/all_gather | solution.py:99
  34.2 117.2 %all-gather.16.cloned.1.call-start = ((), (), s32[]{:S(2)}) async-start(), calls=%async_computation.5 | async-start | bytes 2359296 | tf_op jit(solution)/shard_map/all_gather | solution.py:100
  34.2 10.9 %copy-start.4 = (bf16[3,3,16,32]{3,2,1,0:T(8,128)(2,1)S(1)}, bf16[3,3,16,32]{3,2,1,0:T(8,128)(2,1)}, u32[]{:S(2)}) copy-start(bf16[3,3,16,32]{3,2,1,0:T(8,128)(2,1)} %param.12) | copy-start | bytes 27652
  34.2 10.9 %copy-start.5 = (bf16[3,3,1,16]{3,1,2,0:T(4,128)(2,1)S(1)}, bf16[3,3,1,16]{3,1,2,0:T(4,128)(2,1)}, u32[]{:S(2)}) copy-start(bf16[3,3,1,16]{3,1,2,0:T(4,128)(2,1)} %param.11) | copy-start | bytes 868
  53.2 8.5 %copy-start.3 = (f32[2,3,512]{2,0,1:T(2,128)S(1)}, f32[2,3,512]{2,0,1:T(2,128)}, u32[]{:S(2)}) copy-start(f32[2,3,512]{2,0,1:T(2,128)} %param.13) | copy-start | bytes 36868
  56.8 5.2 %collective-permute-start = (bf16[32,1,512]{2,0,1:T(8,128)(2,1)S(1)}, bf16[32,1,512]{2,0,1:T(8,128)(2,1)S(1)}, u32[]{:S(2)}, u32[]{:S(2)}) collective-permute-start(bf16[32,1,512]{2,0,1:T(8,128)(2,1)S(1)} %fusion.117), channel_id=1, source_target_pairs={{0,4},{4,8},{8,12},{1,5},{5,9},{9,13},{2,6},{6,10},{10,14},{3,7},{... | collective-permute-start | bytes 98312 | tf_op jit(solution)/shard_map/ppermute | solution.py:16
  60.4 5.8 %collective-permute-start.1 = (bf16[32,1,512]{2,0,1:T(8,128)(2,1)S(1)}, bf16[32,1,512]{2,0,1:T(8,128)(2,1)S(1)}, u32[]{:S(2)}, u32[]{:S(2)}) collective-permute-start(bf16[32,1,512]{2,0,1:T(8,128)(2,1)S(1)} %fusion.117), channel_id=1, source_target_pairs={{4,0},{8,4},{12,8},{5,1},{9,5},{13,9},{6,2},{10,6},{14,10},{7,3},{... | collective-permute-start | bytes 98312 | tf_op jit(solution)/shard_map/ppermute | solution.py:19
  94.9 4.9 %collective-permute-start.2 = (bf16[32,1,512]{2,0,1:T(8,128)(2,1)S(1)}, bf16[32,1,512]{2,0,1:T(8,128)(2,1)S(1)}, u32[]{:S(2)}, u32[]{:S(2)}) collective-permute-start(bf16[32,1,512]{2,0,1:T(8,128)(2,1)S(1)} %fusion.118), channel_id=1, source_target_pairs={{0,4},{4,8},{8,12},{1,5},{5,9},{9,13},{2,6},{6,10},{10,14},{3,7},{... | collective-permute-start | bytes 98312 | tf_op jit(solution)/shard_map/ppermute | solution.py:16
  98.3 7.2 %collective-permute-start.3 = (bf16[32,1,512]{2,0,1:T(8,128)(2,1)S(1)}, bf16[32,1,512]{2,0,1:T(8,128)(2,1)S(1)}, u32[]{:S(2)}, u32[]{:S(2)}) collective-permute-start(bf16[32,1,512]{2,0,1:T(8,128)(2,1)S(1)} %fusion.118), channel_id=1, source_target_pairs={{4,0},{8,4},{12,8},{5,1},{9,5},{13,9},{6,2},{10,6},{14,10},{7,3},{... | collective-permute-start | bytes 98312 | tf_op jit(solution)/shard_map/ppermute | solution.py:19
Sparse Core Ops, SparseCore 0:
  31.8 6.1 reduce-scatter.1
Sparse Core Ops, SparseCore 1:
  33.8 27.3 all-gather.9
  62.6 28.4 all-gather.11
  92.5 29.5 all-gather.13
  123.6 27.6 all-gather.15
where the time goes:
time: 165 us
  waiting for transfers between devices  85.4 us (52%)
  blocking collectives  22.4 us (14%)
  matrix products  16.4 us (10%)
  between operations  15.3 us (9%)
  local copies, waits for them, and re-layouts  9.7 us (6%)
  starting transfers between devices  9.66 us (6%)
  other arithmetic  6.17 us (4%)
    all_gather x2, waiting for transfers between devices, on_device(): lax.all_gather(w_out[mixer], ('frame', 'chan'), axis=0, tiled=True)  54.1 us
    psum x1, blocking collectives, on_device(): query_vectors = lax.psum(picked.astype(jnp.bfloat16), 'frame')  20.5 us
    all_gather x2, waiting for transfers between devices, on_device(): lax.all_gather(w_in[mixer], ('frame', 'chan'), axis=0, tiled=True)  16.6 us
    ppermute x2, waiting for transfers between devices, padded_2(): lax.ppermute(lax.slice_in_dim(block, 0, width, axis=dim), axis, backward)  9.86 us
    conv_general_dilated x1, matrix products, pool_maps(): lax.conv_general_dilated(first_maps, conv_second, (2, 2), 'SAME', dimensi...  8.04 us
    dot_general x2, matrix products, on_device(): jnp.dot(hidden, out_piece, preferred_element_type=jnp.float32)  7.08 us
    ppermute x2, starting transfers between devices, padded_2(): lax.ppermute(lax.slice_in_dim(block, block.shape[dim] - width, None, axis...  6.9 us
    squeeze x2, local copies, waits for them, and re-layouts, on_device(): lax.map(lambda frame_maps: pool_maps(frame_maps, conv_first, conv_second)...  6.11 us
  transfers between devices with their start and end apart: 9, of which 8 were waited for; matrix products, arithmetic and copies ran while one was open for 15% of the time, Pallas kernels for 0%

commit v1 on v0

v1 whole, which is shorter than its diff:
```python
import functools
import math

import jax
import jax.numpy as jnp
from jax import lax
from jax.experimental import pallas as pl
from jax.experimental.pallas import tpu as pltpu
from jax.sharding import PartitionSpec as P

MESH = pl.DeviceIdType.MESH
F32 = jnp.float32
BF16 = jnp.bfloat16

ERF_TOP = (
    -2.72614225801306e-10,
    2.77068142495902e-08,
    -2.10102402082508e-06,
    -5.69250639462346e-05,
    -7.34990630326855e-04,
    -2.95459980854025e-03,
    -1.60960333262415e-02,
)
ERF_BOTTOM = (
    -1.45660718464996e-05,
    -2.13374055278905e-04,
    -1.68282697438203e-03,
    -7.37332916720468e-03,
    -1.42647390514189e-02,
)


def erf(x):
    x = jnp.clip(x, -4.0, 4.0)
    square = x * x
    top = jnp.full_like(x, ERF_TOP[0])
    for c in ERF_TOP[1:]:
        top = top * square + c
    bottom = jnp.full_like(x, ERF_BOTTOM[0])
    for c in ERF_BOTTOM[1:]:
        bottom = bottom * square + c
    return x * top / bottom


def gelu(x):
    return 0.5 * x * (1.0 + erf(x * math.sqrt(0.5)))


def layer_norm(state):
    centre = state - jnp.mean(state, axis=-1, keepdims=True)
    spread = jnp.mean(centre * centre, axis=-1, keepdims=True)
    return (centre * lax.rsqrt(spread + 1e-05)).astype(BF16)


def iota(shape, dim):
    return lax.broadcasted_iota(jnp.int32, shape, dim)


def log2(n):
    bits = n.bit_length() - 1
    assert 1 << bits == n
    return bits


def kernel(
    frames,
    side,
    corr_scale,
    feat_hbm,
    frame_ref,
    pixel_ref,
    conv1_ref,
    conv2_ref,
    depth_ref,
    win_hbm,
    wout_hbm,
    out_ref,
    feat,
    win,
    wout,
    qsend,
    qall,
    qsum,
    cbuf,
    crecv,
    cme,
    cmo,
    f1e,
    f1o,
    t1,
    t2,
    state,
    hall,
    pbuf,
    precv,
    psend,
    rrecv,
    outbuf,
    local_sem,
    q_send_sem,
    q_recv_sem,
    c_send_sem,
    c_recv_sem,
    g_send_sem,
    g_recv_sem,
    h_send_sem,
    h_recv_sem,
    p_send_sem,
    p_recv_sem,
    r_send_sem,
    r_recv_sem,
    o_send_sem,
    o_recv_sem,
):
    me = lax.axis_index("frame")
    core = lax.axis_index("chan")
    other = 1 - core
    peers = [lax.rem(me + d, frames) for d in range(frames)]
    sources = [lax.rem(me + frames - d, frames) for d in range(frames)]

    feat_copy = pltpu.make_async_copy(feat_hbm, feat, local_sem.at[0])
    feat_copy.start()
    win_copy = pltpu.make_async_copy(win_hbm, win, local_sem.at[1])
    win_copy.start()
    wout_copy = pltpu.make_async_copy(wout_hbm, wout, local_sem.at[2])
    wout_copy.start()

    barrier = pltpu.get_barrier_semaphore()
    for d in range(1, frames):
        pl.semaphore_signal(barrier, inc=1, device_id={"frame": peers[d]}, device_id_type=MESH)
    pl.semaphore_signal(barrier, inc=1, device_id={"chan": other}, device_id_type=MESH)

    queries = qsum.shape[0]
    half = queries // 2
    pixels = side * side
    mixers = win.shape[0]
    tile = 128
    blocks = pixels // tile
    pairs = blocks // 2

    local = jnp.where(
        frame_ref[...] == me, pixel_ref[0:1, :] * side + pixel_ref[1:2, :], -1
    ).astype(F32)
    diag = iota((queries, queries), 0) == iota((queries, queries), 1)
    column = jnp.sum(
        jnp.where(diag, jnp.broadcast_to(local, (queries, queries)), 0.0), axis=1, keepdims=True
    ).astype(jnp.int32)
    feat_copy.wait()
    step = 512
    picked = jnp.zeros((queries, feat.shape[1]), F32)
    lanes = iota((queries, step), 1)
    for k in range(pixels // step):
        hot = (lanes == (column - k * step)).astype(F32).astype(BF16)
        picked += jnp.dot(hot, feat[k * step : (k + 1) * step, :], preferred_element_type=F32)
    qsend[...] = picked.astype(BF16)

    pl.semaphore_wait(barrier, frames)
    q_copies = []
    for d in range(frames - 1, 0, -1):
        copy = pltpu.make_async_remote_copy(
            src_ref=qsend,
            dst_ref=qall.at[d - 1],
            send_sem=q_send_sem.at[d - 1],
            recv_sem=q_recv_sem.at[d - 1],
            device_id={"frame": peers[d]},
            device_id_type=MESH,
        )
        copy.start()
        q_copies.append(copy)

    c1 = conv1_ref.shape[1]
    c2 = conv2_ref.shape[1]
    wide = (side // 2) * c1
    spread1 = (iota((c1, wide), 0) == (iota((c1, wide), 1) & (c1 - 1))).astype(F32).astype(BF16)
    rows1 = jnp.dot(conv1_ref[...], spread1, preferred_element_type=F32)
    offset = iota((side, wide), 0) - 2 * (iota((side, wide), 1) >> log2(c1))
    for a in range(3):
        band = jnp.zeros((side, wide), F32)
        for b in range(3):
            band = jnp.where(offset == b, rows1[3 * a + b : 3 * a + b + 1, :], band)
        t1[a * side : (a + 1) * side, :] = band.astype(BF16)
    t1[3 * side :, :] = jnp.zeros((t1.shape[0] - 3 * side, wide), BF16)
    spread2 = (iota((c2, tile), 0) == (iota((c2, tile), 1) & (c2 - 1))).astype(F32).astype(BF16)
    rows2 = jnp.dot(conv2_ref[...], spread2, preferred_element_type=F32)
    cells = 2 * tile // c1
    offset = iota((cells, c1, tile), 0) - 2 * (iota((cells, c1, tile), 2) >> log2(c2))
    for a in range(3):
        band = jnp.zeros((cells, c1, tile), F32)
        for b in range(3):
            start = (3 * a + b) * c1
            band = jnp.where(offset == b, rows2[start : start + c1, :][None], band)
        t2[a] = band.reshape(cells * c1, tile).astype(BF16)
    cme[pairs] = jnp.zeros((half, tile), BF16)
    f1e[pairs] = jnp.zeros((half, f1e.shape[2]), BF16)
    f1e[:, :, wide:] = jnp.zeros((f1e.shape[0], half, tile), BF16)
    f1o[:, :, wide:] = jnp.zeros((f1o.shape[0], half, tile), BF16)

    total = qsend[...].astype(F32)
    for copy in q_copies:
        copy.wait()
    for d in range(1, frames):
        total += qall[d - 1].astype(F32)
    vectors = total.astype(BF16)

    chunks = c_send_sem.shape[0]
    per = blocks // chunks
    c_copies = []
    for k in range(chunks):
        corr = lax.dot_general(
            vectors,
            feat[k * per * tile : (k + 1) * per * tile, :],
            (((1,), (1,)), ((), ())),
            preferred_element_type=F32,
        ).astype(BF16)
        for h in range(2):
            for i in range(per):
                cbuf[h, k * per + i] = corr[h * half : (h + 1) * half, i * tile : (i + 1) * tile]
        copy = pltpu.make_async_remote_copy(
            src_ref=cbuf.at[other, pl.ds(k * per, per)],
            dst_ref=crecv.at[pl.ds(k * per, per)],
            send_sem=c_send_sem.at[k],
            recv_sem=c_recv_sem.at[k],
            device_id={"chan": other},
            device_id_type=MESH,
        )
        copy.start()
        c_copies.append(copy)
    for k in range(chunks):
        c_copies[k].wait()
        for i in range(k * per, (k + 1) * per):
            summed = cbuf[core, i].astype(F32) + crecv[i].astype(F32)
            value = (summed * corr_scale).astype(BF16)
            if i % 2 == 0:
                cme[i // 2] = value
            else:
                cmo[i // 2] = value

    window = pairs // 4
    for r in range(0, pairs, window):
        rows = window * half
        even = cme[r : r + window].reshape(rows, tile)
        odd = cmo[r : r + window].reshape(rows, tile)
        after = cme[r + 1 : r + window + 1].reshape(rows, tile)
        for first, second, dest in ((even, odd, f1e), (odd, after, f1o)):
            maps = jnp.dot(
                jnp.concatenate([first, second], axis=1), t1[...], preferred_element_type=F32
            )
            dest[r : r + window, :, :wide] = (
                jnp.maximum(maps, 0.0).astype(BF16).reshape(window, half, wide)
            )
    group = iota((half, tile), 1) >> log2(c2)
    cols = wide // tile
    for r in range(0, pairs, window):
        rows = window * half
        packed = jnp.zeros((half, tile), F32)
        for u in range(cols):
            span = slice(u * tile, (u + 2) * tile)
            maps = jnp.dot(
                f1e[r : r + window, :, span].reshape(rows, 2 * tile),
                t2[0],
                preferred_element_type=F32,
            )
            maps += jnp.dot(
                f1o[r : r + window, :, span].reshape(rows, 2 * tile),
                t2[1],
                preferred_element_type=F32,
            )
            maps += jnp.dot(
                f1e[r + 1 : r + window + 1, :, span].reshape(rows, 2 * tile),
                t2[2],
                preferred_element_type=F32,
            )
            pooled = jnp.sum(jnp.maximum(maps, 0.0).reshape(window, half, tile), axis=0)
            pooled = pooled + pltpu.roll(pooled, tile // 2, 1)
            pooled = pooled + pltpu.roll(pooled, c2, 1)
            packed = jnp.where(group == u, pooled, packed)
        part = r // window
        state[:, part * tile : (part + 1) * tile] = packed * (1.0 / (window * window))

    pending = []
    for m in range(mixers):
        normed = layer_norm(state[...])
        hall[m, me, core] = normed
        mine = hall.at[m, me, core]
        g_copies = {}
        for d in range(frames - 1, 0, -1):
            copy = pltpu.make_async_remote_copy(
                src_ref=mine,
                dst_ref=mine,
                send_sem=g_send_sem.at[m, d - 1],
                recv_sem=g_recv_sem.at[m, d - 1],
                device_id={"frame": peers[d]},
                device_id_type=MESH,
            )
            copy.start()
            g_copies[d] = copy
        h_copies = []
        for d in range(frames):
            if d:
                g_copies[d].wait_recv()
            block = hall.at[m, sources[d], core]
            copy = pltpu.make_async_remote_copy(
                src_ref=block,
                dst_ref=block,
                send_sem=h_send_sem.at[m, d],
                recv_sem=h_recv_sem.at[m, d],
                device_id={"chan": other},
                device_id_type=MESH,
            )
            copy.start()
            h_copies.append(copy)
        for copy in h_copies:
            copy.wait()
        for copy in g_copies.values():
            copy.wait_send()
        if m == 0:
            win_copy.wait()
            wout_copy.wait()
        width = hall.shape[4]
        taps = [depth_ref[m, j : j + 1, :] for j in range(3)]
        blocks_of = [hall[m, f].reshape(queries, width).astype(F32) for f in range(frames)]
        zero = jnp.zeros((queries, width), F32)
        p_copies = []
        for f in range(frames):
            before = blocks_of[f - 1] if f else zero
            behind = blocks_of[f + 1] if f + 1 < frames else zero
            mixed = (taps[0] * before + taps[1] * blocks_of[f] + taps[2] * behind).astype(BF16)
            pre = lax.dot_general(
                mixed, win[m], (((1,), (1,)), ((), ())), preferred_element_type=F32
            )
            hidden = gelu(pre).astype(BF16)
            update = jnp.dot(hidden, wout[m], preferred_element_type=F32).astype(BF16)
            pbuf[m, f] = update.reshape(2, half, width)
            copy = pltpu.make_async_remote_copy(
                src_ref=pbuf.at[m, f, other],
                dst_ref=precv.at[m, f],
                send_sem=p_send_sem.at[m, f],
                recv_sem=p_recv_sem.at[m, f],
                device_id={"chan": other},
                device_id_type=MESH,
            )
            copy.start()
            p_copies.append(copy)
        for copy in p_copies:
            copy.wait()
        r_copies = []
        for d in range(frames - 1, 0, -1):
            psend[m, d] = (
                pbuf[m, peers[d], core].astype(F32) + precv[m, peers[d]].astype(F32)
            ).astype(BF16)
            copy = pltpu.make_async_remote_copy(
                src_ref=psend.at[m, d],
                dst_ref=rrecv.at[m, d - 1],
                send_sem=r_send_sem.at[m, d - 1],
                recv_sem=r_recv_sem.at[m, d - 1],
                device_id={"frame": peers[d]},
                device_id_type=MESH,
            )
            copy.start()
            r_copies.append(copy)
        total = pbuf[m, me, core].astype(F32) + precv[m, me].astype(F32)
        for copy in r_copies:
            copy.wait()
        for d in range(1, frames):
            total += rrecv[m, d - 1].astype(F32)
        state[...] = state[...] + total

    outbuf[core] = state[...].astype(BF16)
    copy = pltpu.make_async_remote_copy(
        src_ref=outbuf.at[core],
        dst_ref=outbuf.at[core],
        send_sem=o_send_sem,
        recv_sem=o_recv_sem,
        device_id={"chan": other},
        device_id_type=MESH,
    )
    copy.start()
    copy.wait()
    out_ref[...] = outbuf[...].reshape(queries, outbuf.shape[2])


def on_device(
    features, query_frame, query_pixel, conv_first, conv_second, depth_kernel, w_in, w_out
):
    frames = lax.axis_size("frame")
    chans = lax.axis_size("chan")
    local_frames, side, _, chan_width = features.shape
    queries = query_frame.shape[0]
    mixers, hidden, width = w_in.shape
    c1 = conv_first.shape[3]
    c2 = conv_second.shape[3]
    half = queries // 2
    pixels = side * side
    blocks = pixels // 128
    wide = side // 2 * c1
    assert local_frames == 1 and chans == 2 and side == 64 and wide == width == 16 * c2
    any_space = pl.BlockSpec(memory_space=pl.ANY)
    vmem = pl.BlockSpec(memory_space=pltpu.VMEM)
    dma = pltpu.SemaphoreType.DMA
    chunks = 4
    out = pl.pallas_call(
        functools.partial(kernel, frames, side, 1.0 / math.sqrt(chan_width * chans)),
        out_shape=jax.ShapeDtypeStruct((queries, width), BF16),
        in_specs=[any_space, vmem, vmem, vmem, vmem, vmem, any_space, any_space],
        out_specs=vmem,
        scratch_shapes=[
            pltpu.VMEM((pixels, chan_width), BF16),
            pltpu.VMEM((mixers, hidden, width), BF16),
            pltpu.VMEM((mixers, hidden, width), BF16),
            pltpu.VMEM((queries, chan_width), BF16),
            pltpu.VMEM((frames - 1, queries, chan_width), BF16),
            pltpu.VMEM((queries, chan_width), BF16),
            pltpu.VMEM((2, blocks, half, 128), BF16),
            pltpu.VMEM((blocks, half, 128), BF16),
            pltpu.VMEM((blocks // 2 + 1, half, 128), BF16),
            pltpu.VMEM((blocks // 2, half, 128), BF16),
            pltpu.VMEM((blocks // 2 + 1, half, wide + 128), BF16),
            pltpu.VMEM((blocks // 2, half, wide + 128), BF16),
            pltpu.VMEM((4 * side, wide), BF16),
            pltpu.VMEM((3, 256, 128), BF16),
            pltpu.VMEM((half, width), F32),
            pltpu.VMEM((mixers, frames, 2, half, width), BF16),
            pltpu.VMEM((mixers, frames, 2, half, width), BF16),
            pltpu.VMEM((mixers, frames, half, width), BF16),
            pltpu.VMEM((mixers, frames, half, width), BF16),
            pltpu.VMEM((mixers, frames - 1, half, width), BF16),
            pltpu.VMEM((2, half, width), BF16),
            dma((3,)),
            dma((frames - 1,)),
            dma((frames - 1,)),
            dma((chunks,)),
            dma((chunks,)),
            dma((mixers, frames - 1)),
            dma((mixers, frames - 1)),
            dma((mixers, frames)),
            dma((mixers, frames)),
            dma((mixers, frames)),
            dma((mixers, frames)),
            dma((mixers, frames - 1)),
            dma((mixers, frames - 1)),
            dma,
            dma,
        ],
        compiler_params=pltpu.CompilerParams(
            collective_id=0, has_side_effects=True, vmem_limit_bytes=48 * 1024 * 1024
        ),
        name="track_step",
    )(
        features.reshape(pixels, chan_width),
        query_frame.reshape(1, queries),
        query_pixel.T,
        conv_first.reshape(9, c1),
        conv_second.reshape(9 * c1, c2),
        depth_kernel,
        w_in,
        w_out,
    )
    return out.reshape(queries, 1, width)


def solution(mesh):
    in_specs = (
        P(("groups", "frame"), None, None, "chan"),
        P(("groups", "query")),
        P(("groups", "query"), None),
        P(),
        P(),
        P(),
        P(None, ("frame", "chan"), None),
        P(None, ("frame", "chan"), None),
    )
    out_specs = P(("groups", "query"), "frame", None)
    return jax.shard_map(
        on_device, mesh=mesh, in_specs=in_specs, out_specs=out_specs, check_vma=False
    )
```

time: 165 us -> 46.2 us (0.28)
  waiting for transfers between devices: 85.4 us -> 0 us
  Pallas kernels: 0 us -> 40.4 us
  blocking collectives: 22.4 us -> 0 us
  matrix products: 16.4 us -> 0 us
  between operations: 15.3 us -> 0.03 us
  starting transfers between devices: 9.66 us -> 0 us
  other arithmetic: 6.17 us -> 0 us
  local copies, waits for them, and re-layouts: 9.7 us -> 5.39 us
    all_gather x4 -> x0, waiting for transfers between devices: 70.6 us -> none  [the longest x2 54.1 us: on_device(): lax.all_gather(w_out[mixer], ('frame', 'chan'), axis=0, tiled=True)]
    pallas_call x0 -> x1, Pallas kernels: none -> 40.4 us  [on_device(): pl.pallas_call(functools.partial(kernel, frames, side, 1.0 / math.sqrt(ch...]
    psum x1 -> x0, blocking collectives: 20.5 us -> none  [on_device(): query_vectors = lax.psum(picked.astype(jnp.bfloat16), 'frame')]
    ppermute x4 -> x0, waiting for transfers between devices: 10.4 us -> none  [the longest x2 9.86 us: padded_2(): lax.ppermute(lax.slice_in_dim(block, 0, width, axis=dim), axis, backward)]
    ppermute x4 -> x0, starting transfers between devices: 9.48 us -> none  [the longest x2 6.9 us: padded_2(): lax.ppermute(lax.slice_in_dim(block, block.shape[dim] - width, None, axis...]
    dot_general x3 -> x0, matrix products: 8.36 us -> none  [the longest x2 7.08 us: on_device(): jnp.dot(hidden, out_piece, preferred_element_type=jnp.float32)]
    conv_general_dilated x1 -> x0, matrix products: 8.04 us -> none  [pool_maps(): lax.conv_general_dilated(first_maps, conv_second, (2, 2), 'SAME', dimensi...]
    squeeze x2 -> x0, local copies, waits for them, and re-layouts: 6.11 us -> none  [on_device(): lax.map(lambda frame_maps: pool_maps(frame_maps, conv_first, conv_second)...]
  transfers between devices with their start and end apart: 9 -> 0, of which waited for: 8 -> 0; matrix products, arithmetic and copies ran while one was open for 15% -> 0% of each run, Pallas kernels for 0% -> 0%
where the time goes in v1:
time: 46.2 us; the launch traced here: 45.8 us
  Pallas kernels  40.4 us (87%)
  local copies, waits for them, and re-layouts  5.39 us (12%)
    pallas_call x1, Pallas kernels, on_device(): pl.pallas_call(functools.partial(kernel, frames, side, 1.0 / math.sqrt(ch...  40.4 us
    unnamed x14, local copies, waits for them, and re-layouts  4.68 us

profile of v1, /device:TPU:0, one launch (start us, length us, event | category | flops | bytes accessed | tf_op | source)
XLA Modules:
  0.0 45.8 jit_solution(17590556410483880882)
XLA Ops:
  0.0 0.0 copy-start.3
  0.0 0.7 %reshape.17.conv1_ref = bf16[9,16]{1,0:T(8,128)(2,1)S(1)} reshape(bf16[3,3,1,16]{3,1,2,0:T(4,128)(2,1)} %param.11) | data formatting | bytes 576 | tf_op jit(solution)/shard_map/reshape | solution.py:452
  0.7 0.0 copy-start.4
  0.7 0.0 copy-start.5
  0.7 0.7 %copy.9.depth_ref = f32[2,3,512]{2,1,0:T(4,128)S(1)} copy(f32[2,3,512]{2,0,1:T(2,128)} %param.13) | data formatting | bytes 24576 | tf_op args[5]
  1.5 0.0 copy-done.3
  1.5 0.0 copy-done.4
  1.5 0.0 copy-done.5
  1.5 0.0 copy-start
  1.5 1.2 %copy-done = bf16[1,64,64,128]{3,2,1,0:T(8,128)(2,1)S(1)} copy-done((bf16[1,64,64,128]{3,2,1,0:T(8,128)(2,1)S(1)}, bf16[1,64,64,128]{3,2,1,0:T(8,128)(2,1)}, u32[]{:S(2)}) %copy-start) | copy-done | bytes 1048600
  2.7 0.0 copy-start.1
  2.7 1.0 %copy-done.1 = bf16[2,256,512]{2,1,0:T(8,128)(2,1)S(1)} copy-done((bf16[2,256,512]{2,1,0:T(8,128)(2,1)S(1)}, bf16[2,256,512]{2,1,0:T(8,128)(2,1)}, u32[]{:S(2)}) %copy-start.1) | copy-done | bytes 524312
  3.7 0.0 copy-start.2
  3.7 1.0 %copy-done.2 = bf16[2,256,512]{2,1,0:T(8,128)(2,1)S(1)} copy-done((bf16[2,256,512]{2,1,0:T(8,128)(2,1)S(1)}, bf16[2,256,512]{2,1,0:T(8,128)(2,1)}, u32[]{:S(2)}) %copy-start.2) | copy-done | bytes 524312
  4.8 40.4 %track_step.1 = bf16[64,512]{1,0:T(8,128)(2,1)S(1)} custom-call(bf16[4096,128]{1,0:T(8,128)(2,1)S(1)} %bitcast.7, s32[1,64]{1,0:T(1,128)S(1)} %bitcast.11, s32[2,64]{1,0:T(2,128)S(1)} %bitcast.10, bf16[9,16]{1,0:T(8,128)(2,1)S(1)} %reshape.17.conv1_ref, bf16[144,32]{1,0:T(8,128)(2,1)S(1)} %bitcast.9, f32[2,3,512]{2,1,0:T(4,128)S(1)} %copy.9.depth_ref, ...), custom_call_target="tpu_custom_call" | custom-call | tf_op jit(solution)/shard_map/track_step/pallas_call | solution.py:401
  45.2 0.6 %copy.11 = bf16[64,1,512]{2,0,1:T(8,128)(2,1)} copy(bf16[64,1,512]{2,0,1:T(8,128)(2,1)S(1)} %bitcast.8) | data formatting | bytes 131072
Async XLA Ops:
  0.0 1.5 %copy-start.3 = (bf16[3,3,16,32]{3,2,1,0:T(8,128)(2,1)S(1)}, bf16[3,3,16,32]{3,2,1,0:T(8,128)(2,1)}, u32[]{:S(2)}) copy-start(bf16[3,3,16,32]{3,2,1,0:T(8,128)(2,1)} %param.12) | copy-start | bytes 27652
  0.7 0.7 %copy-start.4 = (s32[64,2]{0,1:T(2,128)S(1)}, s32[64,2]{0,1:T(2,128)}, u32[]{:S(2)}) copy-start(s32[64,2]{0,1:T(2,128)} %param.10) | copy-start | bytes 1540
  0.7 0.8 %copy-start.5 = (s32[64]{0:T(128)S(1)}, s32[64]{0:T(128)}, u32[]{:S(2)}) copy-start(s32[64]{0:T(128)} %param.9) | copy-start | bytes 772
  1.5 1.2 %copy-start = (bf16[1,64,64,128]{3,2,1,0:T(8,128)(2,1)S(1)}, bf16[1,64,64,128]{3,2,1,0:T(8,128)(2,1)}, u32[]{:S(2)}) copy-start(bf16[1,64,64,128]{3,2,1,0:T(8,128)(2,1)} %param.8) | copy-start | bytes 3145732
  2.7 1.0 %copy-start.1 = (bf16[2,256,512]{2,1,0:T(8,128)(2,1)S(1)}, bf16[2,256,512]{2,1,0:T(8,128)(2,1)}, u32[]{:S(2)}) copy-start(bf16[2,256,512]{2,1,0:T(8,128)(2,1)} %win_hbm.1) | copy-start | bytes 1572868
  3.7 1.0 %copy-start.2 = (bf16[2,256,512]{2,1,0:T(8,128)(2,1)S(1)}, bf16[2,256,512]{2,1,0:T(8,128)(2,1)}, u32[]{:S(2)}) copy-start(bf16[2,256,512]{2,1,0:T(8,128)(2,1)} %wout_hbm.1) | copy-start | bytes 1572868

commit v2 on v1

--- a/solution.py
+++ b/solution.py
@@ -92,8 +92,6 @@
     state,
     hall,
     pbuf,
-    precv,
-    psend,
     rrecv,
     outbuf,
     local_sem,
@@ -103,10 +101,8 @@
     c_recv_sem,
     g_send_sem,
     g_recv_sem,
-    h_send_sem,
-    h_recv_sem,
-    p_send_sem,
-    p_recv_sem,
+    w_send_sem,
+    w_recv_sem,
     r_send_sem,
     r_recv_sem,
     o_send_sem,
@@ -120,10 +116,12 @@
 
     feat_copy = pltpu.make_async_copy(feat_hbm, feat, local_sem.at[0])
     feat_copy.start()
-    win_copy = pltpu.make_async_copy(win_hbm, win, local_sem.at[1])
-    win_copy.start()
-    wout_copy = pltpu.make_async_copy(wout_hbm, wout, local_sem.at[2])
-    wout_copy.start()
+    w_copies = [
+        pltpu.make_async_copy(win_hbm, win.at[core], local_sem.at[1]),
+        pltpu.make_async_copy(wout_hbm, wout.at[core], local_sem.at[2]),
+    ]
+    for copy in w_copies:
+        copy.start()
 
     barrier = pltpu.get_barrier_semaphore()
     for d in range(1, frames):
@@ -133,7 +131,7 @@
     queries = qsum.shape[0]
     half = queries // 2
     pixels = side * side
-    mixers = win.shape[0]
+    mixers = win.shape[1]
     tile = 128
     blocks = pixels // tile
     pairs = blocks // 2
@@ -168,16 +166,28 @@
         copy.start()
         q_copies.append(copy)
 
-    c1 = conv1_ref.shape[1]
+    for j, (source, dest) in enumerate(((win_hbm, win), (wout_hbm, wout))):
+        copy = pltpu.make_async_remote_copy(
+            src_ref=source,
+            dst_ref=dest.at[core],
+            send_sem=w_send_sem.at[j],
+            recv_sem=w_recv_sem.at[j],
+            device_id={"chan": other},
+            device_id_type=MESH,
+        )
+        copy.start()
+        w_copies.append(copy)
+
+    c1 = conv1_ref.shape[2]
     c2 = conv2_ref.shape[1]
     wide = (side // 2) * c1
     spread1 = (iota((c1, wide), 0) == (iota((c1, wide), 1) & (c1 - 1))).astype(F32).astype(BF16)
-    rows1 = jnp.dot(conv1_ref[...], spread1, preferred_element_type=F32)
     offset = iota((side, wide), 0) - 2 * (iota((side, wide), 1) >> log2(c1))
     for a in range(3):
+        rows1 = jnp.dot(conv1_ref[a], spread1, preferred_element_type=F32)
         band = jnp.zeros((side, wide), F32)
         for b in range(3):
-            band = jnp.where(offset == b, rows1[3 * a + b : 3 * a + b + 1, :], band)
+            band = jnp.where(offset == b, rows1[b : b + 1, :], band)
         t1[a * side : (a + 1) * side, :] = band.astype(BF16)
     t1[3 * side :, :] = jnp.zeros((t1.shape[0] - 3 * side, wide), BF16)
     spread2 = (iota((c2, tile), 0) == (iota((c2, tile), 1) & (c2 - 1))).astype(F32).astype(BF16)
@@ -277,11 +287,10 @@
         part = r // window
         state[:, part * tile : (part + 1) * tile] = packed * (1.0 / (window * window))
 
-    pending = []
     for m in range(mixers):
         normed = layer_norm(state[...])
-        hall[m, me, core] = normed
-        mine = hall.at[m, me, core]
+        hall[m, me] = normed
+        mine = hall.at[m, me]
         g_copies = {}
         for d in range(frames - 1, 0, -1):
             copy = pltpu.make_async_remote_copy(
@@ -294,62 +303,35 @@
             )
             copy.start()
             g_copies[d] = copy
-        h_copies = []
-        for d in range(frames):
-            if d:
-                g_copies[d].wait_recv()
-            block = hall.at[m, sources[d], core]
-            copy = pltpu.make_async_remote_copy(
-                src_ref=block,
-                dst_ref=block,
-                send_sem=h_send_sem.at[m, d],
-                recv_sem=h_recv_sem.at[m, d],
-                device_id={"chan": other},
-                device_id_type=MESH,
-            )
-            copy.start()
-            h_copies.append(copy)
-        for copy in h_copies:
+        for copy in g_copies.values():
             copy.wait()
-        for copy in g_copies.values():
-            copy.wait_send()
         if m == 0:
-            win_copy.wait()
-            wout_copy.wait()
-        width = hall.shape[4]
-        taps = [depth_ref[m, j : j + 1, :] for j in range(3)]
-        blocks_of = [hall[m, f].reshape(queries, width).astype(F32) for f in range(frames)]
-        zero = jnp.zeros((queries, width), F32)
-        p_copies = []
+            for copy in w_copies:
+                copy.wait()
+        width = hall.shape[3]
+        taps = [depth_ref[j, m : m + 1, :] for j in range(3)]
+        blocks_of = [hall[m, f].astype(F32) for f in range(frames)]
+        zero = jnp.zeros((half, width), F32)
+        mixed = []
         for f in range(frames):
             before = blocks_of[f - 1] if f else zero
             behind = blocks_of[f + 1] if f + 1 < frames else zero
-            mixed = (taps[0] * before + taps[1] * blocks_of[f] + taps[2] * behind).astype(BF16)
+            mixed.append(
+                (taps[0] * before + taps[1] * blocks_of[f] + taps[2] * behind).astype(BF16)
+            )
+        mixed = jnp.concatenate(mixed, axis=0)
+        update = jnp.zeros((frames * half, width), F32)
+        for c in range(2):
             pre = lax.dot_general(
-                mixed, win[m], (((1,), (1,)), ((), ())), preferred_element_type=F32
+                mixed, win[c, m], (((1,), (1,)), ((), ())), preferred_element_type=F32
             )
             hidden = gelu(pre).astype(BF16)
-            update = jnp.dot(hidden, wout[m], preferred_element_type=F32).astype(BF16)
-            pbuf[m, f] = update.reshape(2, half, width)
-            copy = pltpu.make_async_remote_copy(
-                src_ref=pbuf.at[m, f, other],
-                dst_ref=precv.at[m, f],
-                send_sem=p_send_sem.at[m, f],
-                recv_sem=p_recv_sem.at[m, f],
-                device_id={"chan": other},
-                device_id_type=MESH,
-            )
-            copy.start()
-            p_copies.append(copy)
-        for copy in p_copies:
-            copy.wait()
+            update += jnp.dot(hidden, wout[c, m], preferred_element_type=F32)
+        pbuf[m] = update.astype(BF16).reshape(frames, half, width)
         r_copies = []
         for d in range(frames - 1, 0, -1):
-            psend[m, d] = (
-                pbuf[m, peers[d], core].astype(F32) + precv[m, peers[d]].astype(F32)
-            ).astype(BF16)
             copy = pltpu.make_async_remote_copy(
-                src_ref=psend.at[m, d],
+                src_ref=pbuf.at[m, peers[d]],
                 dst_ref=rrecv.at[m, d - 1],
                 send_sem=r_send_sem.at[m, d - 1],
                 recv_sem=r_recv_sem.at[m, d - 1],
@@ -358,12 +340,12 @@
             )
             copy.start()
             r_copies.append(copy)
-        total = pbuf[m, me, core].astype(F32) + precv[m, me].astype(F32)
+        total = state[...] + pbuf[m, me].astype(F32)
         for copy in r_copies:
             copy.wait()
         for d in range(1, frames):
             total += rrecv[m, d - 1].astype(F32)
-        state[...] = state[...] + total
+        state[...] = total
 
     outbuf[core] = state[...].astype(BF16)
     copy = pltpu.make_async_remote_copy(
@@ -405,8 +387,8 @@
         out_specs=vmem,
         scratch_shapes=[
             pltpu.VMEM((pixels, chan_width), BF16),
-            pltpu.VMEM((mixers, hidden, width), BF16),
-            pltpu.VMEM((mixers, hidden, width), BF16),
+            pltpu.VMEM((2, mixers, hidden, width), BF16),
+            pltpu.VMEM((2, mixers, hidden, width), BF16),
             pltpu.VMEM((queries, chan_width), BF16),
             pltpu.VMEM((frames - 1, queries, chan_width), BF16),
             pltpu.VMEM((queries, chan_width), BF16),
@@ -419,8 +401,6 @@
             pltpu.VMEM((4 * side, wide), BF16),
             pltpu.VMEM((3, 256, 128), BF16),
             pltpu.VMEM((half, width), F32),
-            pltpu.VMEM((mixers, frames, 2, half, width), BF16),
-            pltpu.VMEM((mixers, frames, 2, half, width), BF16),
             pltpu.VMEM((mixers, frames, half, width), BF16),
             pltpu.VMEM((mixers, frames, half, width), BF16),
             pltpu.VMEM((mixers, frames - 1, half, width), BF16),
@@ -432,26 +412,24 @@
             dma((chunks,)),
             dma((mixers, frames - 1)),
             dma((mixers, frames - 1)),
-            dma((mixers, frames)),
-            dma((mixers, frames)),
-            dma((mixers, frames)),
-            dma((mixers, frames)),
+            dma((2,)),
+            dma((2,)),
             dma((mixers, frames - 1)),
             dma((mixers, frames - 1)),
             dma,
             dma,
         ],
         compiler_params=pltpu.CompilerParams(
-            collective_id=0, has_side_effects=True, vmem_limit_bytes=48 * 1024 * 1024
+            collective_id=0, has_side_effects=True
         ),
         name="track_step",
     )(
         features.reshape(pixels, chan_width),
         query_frame.reshape(1, queries),
         query_pixel.T,
-        conv_first.reshape(9, c1),
+        conv_first.transpose(0, 2, 1, 3).reshape(3, 3, c1),
         conv_second.reshape(9 * c1, c2),
-        depth_kernel,
+        depth_kernel.transpose(1, 0, 2),
         w_in,
         w_out,
     )

time: 46.2 us -> 35.4 us (0.77)
  Pallas kernels: 40.4 us -> 33.7 us
  local copies, waits for them, and re-layouts: 5.39 us -> 1.47 us
    pallas_call x1, Pallas kernels: 40.4 us -> 33.7 us  [on_device(): pl.pallas_call(functools.partial(kernel, frames, side, 1.0 / math.sqrt(ch...]
    unnamed x14 -> x1, local copies, waits for them, and re-layouts: 4.68 us -> 1.47 us
    reshape x1 -> x0, local copies, waits for them, and re-layouts: 0.71 us -> none  [on_device(): conv_first.reshape(9, c1)]
where the time goes in v2:
time: 35.4 us; the launch traced here: 35.1 us
  Pallas kernels  33.7 us (95%)
  local copies, waits for them, and re-layouts  1.47 us (4%)
    pallas_call x1, Pallas kernels, on_device(): pl.pallas_call(functools.partial(kernel, frames, side, 1.0 / math.sqrt(ch...  33.7 us
    unnamed x1, local copies, waits for them, and re-layouts  1.47 us

profile of v2, /device:TPU:0, one launch (start us, length us, event | category | flops | bytes accessed | tf_op | source)
XLA Modules:
  0.0 35.1 jit_solution(7598723666350212831)
XLA Ops:
  0.0 33.7 %track_step.1 = bf16[64,512]{1,0:T(8,128)(2,1)} custom-call(bf16[4096,128]{1,0:T(8,128)(2,1)} %bitcast.7, s32[1,64]{1,0:T(1,128)} %bitcast.13, s32[2,64]{1,0:T(2,128)} %bitcast.12, bf16[3,3,16]{2,1,0:T(4,128)(2,1)} %bitcast.11, bf16[144,32]{1,0:T(8,128)(2,1)} %bitcast.9, f32[3,2,512]{2,1,0:T(2,128)} %bitcast.10, bf16[2,256,512]{2,1,0:T(8,128)(2,1)} %win_hbm.1, ...), custom_call_target="tpu_custom_call" | custom-call | tf_op jit(solution)/shard_map/track_step/pallas_call | solution.py:383
  33.7 1.5 %copy.10 = bf16[64,1,512]{2,0,1:T(8,128)(2,1)} copy(bf16[64,1,512]{2,0,1:T(8,128)(2,1)} %bitcast.8) | data formatting | bytes 131072

commit v3 on v2

--- a/solution.py
+++ b/solution.py
@@ -112,7 +112,6 @@
     core = lax.axis_index("chan")
     other = 1 - core
     peers = [lax.rem(me + d, frames) for d in range(frames)]
-    sources = [lax.rem(me + frames - d, frames) for d in range(frames)]
 
     feat_copy = pltpu.make_async_copy(feat_hbm, feat, local_sem.at[0])
     feat_copy.start()
@@ -201,6 +200,9 @@
             band = jnp.where(offset == b, rows2[start : start + c1, :][None], band)
         t2[a] = band.reshape(cells * c1, tile).astype(BF16)
     cme[pairs] = jnp.zeros((half, tile), BF16)
+    for m in range(mixers):
+        hall[m, 0] = jnp.zeros(state.shape, BF16)
+        hall[m, frames + 1] = jnp.zeros(state.shape, BF16)
     f1e[pairs] = jnp.zeros((half, f1e.shape[2]), BF16)
     f1e[:, :, wide:] = jnp.zeros((f1e.shape[0], half, tile), BF16)
     f1o[:, :, wide:] = jnp.zeros((f1o.shape[0], half, tile), BF16)
@@ -289,8 +291,8 @@
 
     for m in range(mixers):
         normed = layer_norm(state[...])
-        hall[m, me] = normed
-        mine = hall.at[m, me]
+        hall[m, me + 1] = normed
+        mine = hall.at[m, me + 1]
         g_copies = {}
         for d in range(frames - 1, 0, -1):
             copy = pltpu.make_async_remote_copy(
@@ -310,41 +312,62 @@
                 copy.wait()
         width = hall.shape[3]
         taps = [depth_ref[j, m : m + 1, :] for j in range(3)]
-        blocks_of = [hall[m, f].astype(F32) for f in range(frames)]
-        zero = jnp.zeros((half, width), F32)
-        mixed = []
-        for f in range(frames):
-            before = blocks_of[f - 1] if f else zero
-            behind = blocks_of[f + 1] if f + 1 < frames else zero
-            mixed.append(
-                (taps[0] * before + taps[1] * blocks_of[f] + taps[2] * behind).astype(BF16)
-            )
-        mixed = jnp.concatenate(mixed, axis=0)
-        update = jnp.zeros((frames * half, width), F32)
-        for c in range(2):
-            pre = lax.dot_general(
-                mixed, win[c, m], (((1,), (1,)), ((), ())), preferred_element_type=F32
-            )
-            hidden = gelu(pre).astype(BF16)
-            update += jnp.dot(hidden, wout[c, m], preferred_element_type=F32)
-        pbuf[m] = update.astype(BF16).reshape(frames, half, width)
         r_copies = []
-        for d in range(frames - 1, 0, -1):
+        for k in range(frames):
+            f = jnp.where(2 * me < frames, frames - 1 - k, k)
+            mixed = (
+                taps[0] * hall[m, f].astype(F32)
+                + taps[1] * hall[m, f + 1].astype(F32)
+                + taps[2] * hall[m, f + 2].astype(F32)
+            ).astype(BF16)
+            update = jnp.zeros((half, width), F32)
+            for c in range(2):
+                pre = lax.dot_general(
+                    mixed, win[c, m], (((1,), (1,)), ((), ())), preferred_element_type=F32
+                )
+                hidden = gelu(pre).astype(BF16)
+                update += jnp.dot(hidden, wout[c, m], preferred_element_type=F32)
+            pbuf[m, k] = update.astype(BF16)
             copy = pltpu.make_async_remote_copy(
-                src_ref=pbuf.at[m, peers[d]],
-                dst_ref=rrecv.at[m, d - 1],
-                send_sem=r_send_sem.at[m, d - 1],
-                recv_sem=r_recv_sem.at[m, d - 1],
-                device_id={"frame": peers[d]},
+                src_ref=pbuf.at[m, k],
+                dst_ref=rrecv.at[m, me],
+                send_sem=r_send_sem.at[m, k],
+                recv_sem=r_recv_sem.at[m, me],
+                device_id={"frame": f},
                 device_id_type=MESH,
             )
-            copy.start()
-            r_copies.append(copy)
-        total = state[...] + pbuf[m, me].astype(F32)
-        for copy in r_copies:
-            copy.wait()
-        for d in range(1, frames):
-            total += rrecv[m, d - 1].astype(F32)
+            r_copies.append((f, copy))
+
+            @pl.when(f != me)
+            def _():
+                copy.start()
+
+            @pl.when(f == me)
+            def _():
+                rrecv[m, me] = pbuf[m, k]
+
+        for f, copy in r_copies:
+
+            @pl.when(f != me)
+            def _():
+                copy.wait_send()
+
+        for source in range(frames):
+
+            @pl.when(source != me)
+            def _():
+                pltpu.make_async_remote_copy(
+                    src_ref=pbuf.at[m, source],
+                    dst_ref=rrecv.at[m, source],
+                    send_sem=r_send_sem.at[m, source],
+                    recv_sem=r_recv_sem.at[m, source],
+                    device_id={"frame": source},
+                    device_id_type=MESH,
+                ).wait_recv()
+
+        total = state[...]
+        for source in range(frames):
+            total += rrecv[m, source].astype(F32)
         state[...] = total
 
     outbuf[core] = state[...].astype(BF16)
@@ -401,9 +424,9 @@
             pltpu.VMEM((4 * side, wide), BF16),
             pltpu.VMEM((3, 256, 128), BF16),
             pltpu.VMEM((half, width), F32),
+            pltpu.VMEM((mixers, frames + 2, half, width), BF16),
             pltpu.VMEM((mixers, frames, half, width), BF16),
             pltpu.VMEM((mixers, frames, half, width), BF16),
-            pltpu.VMEM((mixers, frames - 1, half, width), BF16),
             pltpu.VMEM((2, half, width), BF16),
             dma((3,)),
             dma((frames - 1,)),
@@ -414,8 +437,8 @@
             dma((mixers, frames - 1)),
             dma((2,)),
             dma((2,)),
-            dma((mixers, frames - 1)),
-            dma((mixers, frames - 1)),
+            dma((mixers, frames)),
+            dma((mixers, frames)),
             dma,
             dma,
         ],

time: 35.4 us -> 35.2 us (level)
  no operation moved by 1% of the time
where the time goes in v3:
time: 35.2 us; the launch traced here: 35 us
  Pallas kernels  33.5 us (95%)
  local copies, waits for them, and re-layouts  1.47 us (4%)
    pallas_call x1, Pallas kernels, on_device(): pl.pallas_call(functools.partial(kernel, frames, side, 1.0 / math.sqrt(ch...  33.5 us
    unnamed x1, local copies, waits for them, and re-layouts  1.47 us

profile of v3, /device:TPU:0, one launch (start us, length us, event | category | flops | bytes accessed | tf_op | source)
XLA Modules:
  0.0 35.0 jit_solution(18433254320057973137)
XLA Ops:
  0.0 33.5 %track_step.1 = bf16[64,512]{1,0:T(8,128)(2,1)} custom-call(bf16[4096,128]{1,0:T(8,128)(2,1)} %bitcast.7, s32[1,64]{1,0:T(1,128)} %bitcast.13, s32[2,64]{1,0:T(2,128)} %bitcast.12, bf16[3,3,16]{2,1,0:T(4,128)(2,1)} %bitcast.11, bf16[144,32]{1,0:T(8,128)(2,1)} %bitcast.9, f32[3,2,512]{2,1,0:T(2,128)} %bitcast.10, bf16[2,256,512]{2,1,0:T(8,128)(2,1)} %win_hbm.1, ...), custom_call_target="tpu_custom_call" | custom-call | tf_op jit(solution)/shard_map/track_step/pallas_call | solution.py:406
  33.5 1.5 %copy.10 = bf16[64,1,512]{2,0,1:T(8,128)(2,1)} copy(bf16[64,1,512]{2,0,1:T(8,128)(2,1)} %bitcast.8) | data formatting | bytes 131072
